TPU v7x, 256 devices: a whole 4x4x8 slice. The times are simulated.
256 devices in a mesh: comp: 4 (over z_lo), dom: 64 (over y, x, z_hi, core).
Axes of the slice: x: 4, y: 4, z: 8 (z_hi: 2, z_lo: 4; z = z_hi * 4 + z_lo), core: 2. Of those that a mesh axis runs over, the one named last changes fastest.
Arguments:
- airside_exchange: bfloat16 [4, 4, 65536], P('comp', None, 'dom'), may hold values from -6 to 6
- regrid_matrix_partitions: bfloat16 [4, 512, 4, 128, 128], P('comp', 'dom'), may hold values from -0.25 to 0.25
- regrid_destination_latitude: int32 [4, 512, 4], P('comp', 'dom'), may hold values from 0 to 2047, all different within a row
- thermal_departure: float32 [32, 2048, 128], P(None, ('comp', 'dom')), may hold values from -6 to 6
- diffusivity_coefficient: float32 [31, 2048, 128], P(None, ('comp', 'dom')), may hold values from 0.05 to 3
- elevation_anomaly_profile: float32 [2048, 128], P(('comp', 'dom')), may hold values from -3 to 3
- depth_integrated_volume_flow: float32 [2, 2048, 128], P(None, ('comp', 'dom')), may hold values from -2 to 2
- marine_indicator: int32 [2048, 128], P(('comp', 'dom')), may hold values 0 or 1
Outputs:
- ocean_temperature: float32 [32, 2048, 128], P(None, ('comp', 'dom'))
- ocean_height: float32 [2048, 128], P(('comp', 'dom'))
- atm_surface: bfloat16 [4, 2, 65536], P('comp', None, 'dom')
Inputs may be any that keep to these rules, and one draw needn't show every extreme that they name: `regrid_destination_latitude`: each (section, source block) names 4 different ocean blocks, and every ocean block is named somewhere; ocean block b is grid row b.
All inputs are finite; a program needn't handle non-finite values. No bound on the sum of `marine_indicator` on one device may be relied on, other than what follows from the above.
Results may differ from a plain program's by a relative error of at most 0.0048.
Values may be sent and summed in bfloat16 or wider, within the bound.
No kernel may reach another device: no remote copies, remote signals or barrier semaphores. Data moves between devices by JAX's collectives and lax.ppermute only.
A program may use at most 64 MiB of HBM per device.

v0:
```python
import jax
import jax.numpy as jnp
from jax import lax
from jax.sharding import PartitionSpec as P

NSTEP = 2
NSUB = 8
wave_gain = 0.35
stress_gain = 0.1
fresh_gain = 0.1
spread_gain = 0.2
heating_gain = 0.5


def with_halo(block, sides, width):
    for axis, dim in sides:
        count = lax.axis_size(axis)
        forward = [(i, i + 1) for i in range(count - 1)]
        backward = [(target, source) for source, target in forward]
        low = lax.ppermute(
            lax.slice_in_dim(block, block.shape[dim] - width, None, axis=dim), axis, forward
        )
        high = lax.ppermute(lax.slice_in_dim(block, 0, width, axis=dim), axis, backward)
        block = jnp.concatenate([low, block, high], axis=dim)
    return block


def vertical_solve(explicit, diffusivity_coefficient):
    levels_all = explicit.shape[0]
    solved = []
    ratios = []
    for layer_index in range(levels_all):
        upward = (
            diffusivity_coefficient[layer_index - 1]
            if layer_index > 0
            else jnp.zeros_like(explicit[0])
        )
        downward = (
            diffusivity_coefficient[layer_index]
            if layer_index < levels_all - 1
            else jnp.zeros_like(explicit[0])
        )
        pivots = 1.0 + upward + downward
        if layer_index > 0:
            pivots = pivots - upward * ratios[-1]
            solved.append((explicit[layer_index] + upward * solved[-1]) / pivots)
        else:
            solved.append(explicit[layer_index] / pivots)
        ratios.append(downward / pivots)
    result = [solved[-1]]
    for layer_index in range(levels_all - 2, -1, -1):
        result.append(solved[layer_index] + ratios[layer_index] * result[-1])
    return jnp.stack(result[::-1])


def shards(
    airside_exchange,
    regrid_matrix_partitions,
    regrid_destination_latitude,
    thermal_departure,
    diffusivity_coefficient,
    elevation_anomaly_profile,
    depth_integrated_volume_flow,
    marine_indicator,
):
    groups = lax.axis_size("comp")
    blocks_dom = lax.axis_size("dom")
    rows_here = elevation_anomaly_profile.shape[0]
    width_row = elevation_anomaly_profile.shape[1]
    fields = airside_exchange.shape[1]
    source_blocks = regrid_matrix_partitions.shape[1]
    links = regrid_matrix_partitions.shape[2]
    block_cols = regrid_matrix_partitions.shape[3]
    all_rows = groups * blocks_dom * rows_here
    sources = airside_exchange[0].reshape(fields, source_blocks, block_cols)
    weights = regrid_matrix_partitions[0]
    partial_terms = jnp.einsum(
        "fsa,skab->skfb", sources, weights, preferred_element_type=jnp.float32
    )
    partial_terms = partial_terms.reshape(source_blocks * links, fields, width_row)
    targets = regrid_destination_latitude[0].reshape(-1)
    owner_group = targets // (blocks_dom * rows_here)
    owner_block = targets // rows_here % blocks_dom
    inside_row = targets % rows_here
    placed = owner_block * (groups * rows_here) + owner_group * rows_here + inside_row
    dense_terms = (
        jnp.zeros((all_rows, fields, width_row), jnp.float32).at[placed].add(partial_terms)
    )
    block_sums = lax.psum_scatter(dense_terms, "dom", scatter_dimension=0, tiled=True)
    ocean_flux = lax.psum_scatter(block_sums, "comp", scatter_dimension=0, tiled=True)
    heating = ocean_flux[:, 0, :]
    freshwater = ocean_flux[:, 1, :]
    stress_east = ocean_flux[:, 2, :]
    stress_north = ocean_flux[:, 3, :]
    wet = marine_indicator.astype(jnp.float32)
    face_east = wet * jnp.roll(wet, -1, axis=1)
    height = elevation_anomaly_profile
    flow_east = depth_integrated_volume_flow[0]
    flow_north = depth_integrated_volume_flow[1]
    advected_quantity = thermal_departure
    face_north = None
    for outer_step in range(NSTEP):
        for substep in range(NSUB):
            extended = with_halo(
                jnp.stack([height, flow_north, wet, stress_north]), ((("comp", "dom"), 1),), 1
            )
            edge_height = extended[0]
            edge_north = extended[1]
            edge_wet = extended[2]
            edge_stress = extended[3]
            face_north = edge_wet[:-1] * edge_wet[1:]
            new_east = face_east * (
                flow_east
                - wave_gain * (jnp.roll(height, -1, axis=1) - height)
                + stress_gain * stress_east
            )
            north_rows = face_north * (
                edge_north[:-1]
                - wave_gain * (edge_height[1:] - edge_height[:-1])
                + stress_gain * edge_stress[:-1]
            )
            height = (
                height
                - wave_gain
                * (new_east - jnp.roll(new_east, 1, axis=1) + north_rows[1:] - north_rows[:-1])
                + fresh_gain * freshwater * wet
            )
            flow_east = new_east
            flow_north = north_rows[1:]
        edge_tracer = with_halo(advected_quantity, ((("comp", "dom"), 1),), 1)
        along_east = face_east * (jnp.roll(advected_quantity, -1, axis=2) - advected_quantity)
        along_north = face_north * (edge_tracer[:, 1:] - edge_tracer[:, :-1])
        laplace = (
            along_east - jnp.roll(along_east, 1, axis=2) + along_north[:, 1:] - along_north[:, :-1]
        )
        explicit = advected_quantity + spread_gain * laplace
        explicit = explicit.at[0].add(heating_gain * heating * wet)
        advected_quantity = vertical_solve(explicit, diffusivity_coefficient)
    surface = jnp.stack([advected_quantity[0], height]).astype(jnp.bfloat16)
    shard_rows = lax.all_gather(surface, ("comp", "dom"), axis=1, tiled=True)
    count_rows = shard_rows.shape[1]
    selector = (targets[:, None] == jnp.arange(count_rows, dtype=jnp.int32)[None, :]).astype(
        jnp.bfloat16
    )
    picked = jnp.einsum("nr,frb->nfb", selector, shard_rows, preferred_element_type=jnp.float32)
    chosen = picked.astype(jnp.bfloat16).reshape(source_blocks, links, 2, width_row)
    returned = jnp.einsum("skfb,skab->fsa", chosen, weights, preferred_element_type=jnp.float32)
    return (
        advected_quantity,
        height,
        returned.reshape(1, 2, source_blocks * block_cols).astype(jnp.bfloat16),
    )


def solution(mesh):
    return jax.shard_map(
        shards,
        mesh=mesh,
        in_specs=(
            P("comp", None, "dom"),
            P("comp", "dom", None, None, None),
            P("comp", "dom", None),
            P(None, ("comp", "dom"), None),
            P(None, ("comp", "dom"), None),
            P(("comp", "dom"), None),
            P(None, ("comp", "dom"), None),
            P(("comp", "dom"), None),
        ),
        out_specs=(
            P(None, ("comp", "dom"), None),
            P(("comp", "dom"), None),
            P("comp", None, "dom"),
        ),
        check_vma=False,
    )
```

profile of v0, /device:TPU:1, one launch (start us, length us, event | category | flops | bytes accessed | tf_op | source)
XLA Modules:
  0.0 1094.7 jit_solution(4753517972119351040)
XLA Ops:
  11.7 3.6 scatter_fusion
  15.3 4.5 copy.18
  20.7 5.1 collective-permute-start.16
  25.9 7.0 collective-permute-start.17
  33.1 404.4 %reduce-scatter.3.cloned.1.call-done = f32[32,4,128]{2,0,1:T(8,128)} async-done(((f32[2048,4,128]{2,0,1:T(8,128)}), f32[32,4,128]{2,0,1:T(8,128)}) %reduce-scatter.3.cloned.1.call-update) | async-done | bytes 65552 | tf_op jit(solution)/shard_map/reduce_scatter | solution.py:89
  437.7 26.5 %reduce-scatter.5.cloned.1.call-done = f32[8,4,128]{2,0,1:T(8,128)} async-done(((f32[32,4,128]{2,0,1:T(8,128)}), f32[8,4,128]{2,0,1:T(8,128)}) %reduce-scatter.5.cloned.1.call-update) | async-done | bytes 16400 | tf_op jit(solution)/shard_map/reduce_scatter | solution.py:90
  465.0 7.5 collective-permute-start
  475.5 5.8 collective-permute-done.1
  484.2 2.4 collective-permute-start.3
  487.4 5.6 collective-permute-done.3
  495.1 2.4 collective-permute-start.5
  498.4 5.6 collective-permute-done.5
  506.1 2.4 collective-permute-start.7
  509.4 6.5 collective-permute-done.7
  518.0 2.4 collective-permute-start.9
  521.2 6.5 collective-permute-done.9
  529.9 2.4 collective-permute-start.11
  533.1 6.5 collective-permute-done.11
  541.8 2.4 collective-permute-start.13
  545.0 6.5 collective-permute-done.13
  553.7 2.4 collective-permute-start.15
  556.9 6.5 collective-permute-done.15
  571.4 8.0 collective-permute-start.35
  579.6 2.4 collective-permute-start.20
  584.1 7.6 collective-permute-done.21
  596.5 7.2 collective-permute-done.23
  608.3 7.2 collective-permute-done.25
  620.2 7.2 collective-permute-done.27
  632.1 7.2 collective-permute-done.29
  644.0 7.2 collective-permute-done.31
  655.9 7.6 collective-permute-done.33
  665.6 420.0 %all-gather.2.cloned.1.call-done = bf16[2,2048,128]{2,1,0:T(8,128)(2,1)} async-done(((bf16[2,8,128]{2,1,0:T(8,128)(2,1)}), bf16[2,2048,128]{2,1,0:T(8,128)(2,1)}) %all-gather.2.cloned.1.call-update) | async-done | bytes 1048592 | tf_op jit(solution)/shard_map/all_gather | solution.py:140
  (301 shorter events, 73.4 us)
Async XLA Ops:
  7.2 430.3 %reduce-scatter.3.cloned.1.call-start = ((), (), s32[]{:S(2)}) async-start(), calls=%async_computation.2 | async-start | bytes 4259840 | tf_op jit(solution)/shard_map/reduce_scatter | solution.py:89
  19.9 444.3 %reduce-scatter.5.cloned.1.call-start = ((), (), s32[]{:S(2)}) async-start(), calls=%async_computation.3 | async-start | bytes 81920 | tf_op jit(solution)/shard_map/reduce_scatter | solution.py:90
  20.7 542.7 %collective-permute-start.16 = (f32[32,1,128]{2,1,0:T(1,128)S(1)}, f32[32,1,128]{2,1,0:T(1,128)S(1)}, u32[]{:S(2)}, u32[]{:S(2)}) collective-permute-start(f32[32,1,128]{2,1,0:T(1,128)S(1)} %get-tuple-element.179), channel_id=1, source_target_pairs={{1,0},{2,1},{3,2},{4,3},{5,4},{6,5},{7,6},{8,7},{9,8},{10,9},{11,1... | collective-permute-start | bytes 49160 | tf_op jit(solution)/shard_map/ppermute | solution.py:23
  25.9 537.6 %collective-permute-start.17 = (f32[32,1,128]{2,1,0:T(1,128)S(1)}, f32[32,1,128]{2,1,0:T(1,128)S(1)}, u32[]{:S(2)}, u32[]{:S(2)}) collective-permute-start(f32[32,1,128]{2,1,0:T(1,128)S(1)} %get-tuple-element.178), channel_id=1, source_target_pairs={{0,1},{1,2},{2,3},{3,4},{4,5},{5,6},{6,7},{7,8},{8,9},{9,10},{10,1... | collective-permute-start | bytes 49160 | tf_op jit(solution)/shard_map/ppermute | solution.py:20
  437.5 648.2 %all-gather.2.cloned.1.call-start = ((), (), s32[]{:S(2)}) async-start(), calls=%async_computation.4 | async-start | bytes 1052672 | tf_op jit(solution)/shard_map/all_gather | solution.py:140
  465.0 10.5 collective-permute-start
  472.5 8.8 collective-permute-start.1
  482.2 5.2 collective-permute-start.2
  484.2 8.8 collective-permute-start.3
  493.2 5.2 collective-permute-start.4
  495.1 8.8 collective-permute-start.5
  504.2 5.2 collective-permute-start.6
  506.1 9.7 collective-permute-start.7
  516.1 5.2 collective-permute-start.8
  518.0 9.7 collective-permute-start.9
  528.0 5.2 collective-permute-start.10
  529.9 9.7 collective-permute-start.11
  539.8 5.2 collective-permute-start.12
  541.8 9.7 collective-permute-start.13
  551.7 5.2 collective-permute-start.14
  553.7 9.7 collective-permute-start.15
  564.7 14.6 %collective-permute-start.18 = (f32[4,1,128]{2,1,0:T(1,128)S(1)}, f32[4,1,128]{2,1,0:T(1,128)S(1)}, u32[]{:S(2)}, u32[]{:S(2)}) collective-permute-start(f32[4,1,128]{2,1,0:T(1,128)S(1)} %get-tuple-element.211), channel_id=1, source_target_pairs={{0,1},{1,2},{2,3},{3,4},{4,5},{5,6},{6,7},{7,8},{8,9},{9,10},{10,1... | collective-permute-start | bytes 6152 | tf_op jit(solution)/shard_map/ppermute | solution.py:20
  566.7 12.7 %collective-permute-start.19 = (f32[4,1,128]{2,1,0:T(1,128)S(1)}, f32[4,1,128]{2,1,0:T(1,128)S(1)}, u32[]{:S(2)}, u32[]{:S(2)}) collective-permute-start(f32[4,1,128]{2,1,0:T(1,128)S(1)} %get-tuple-element.210), channel_id=1, source_target_pairs={{1,0},{2,1},{3,2},{4,3},{5,4},{6,5},{7,6},{8,7},{9,8},{10,9},{11,1... | collective-permute-start | bytes 6152 | tf_op jit(solution)/shard_map/ppermute | solution.py:23
  569.4 94.7 %collective-permute-start.34 = (f32[32,1,128]{2,1,0:T(1,128)S(1)}, f32[32,1,128]{2,1,0:T(1,128)S(1)}, u32[]{:S(2)}, u32[]{:S(2)}) collective-permute-start(f32[32,1,128]{2,1,0:T(1,128)S(1)} %get-tuple-element.177), channel_id=1, source_target_pairs={{1,0},{2,1},{3,2},{4,3},{5,4},{6,5},{7,6},{8,7},{9,8},{10,9},{11,1... | collective-permute-start | bytes 49160 | tf_op jit(solution)/shard_map/ppermute | solution.py:23
  571.4 92.8 %collective-permute-start.35 = (f32[32,1,128]{2,1,0:T(1,128)S(1)}, f32[32,1,128]{2,1,0:T(1,128)S(1)}, u32[]{:S(2)}, u32[]{:S(2)}) collective-permute-start(f32[32,1,128]{2,1,0:T(1,128)S(1)} %get-tuple-element.176), channel_id=1, source_target_pairs={{0,1},{1,2},{2,3},{3,4},{4,5},{5,6},{6,7},{7,8},{8,9},{9,10},{10,1... | collective-permute-start | bytes 49160 | tf_op jit(solution)/shard_map/ppermute | solution.py:20
  582.0 9.7 collective-permute-start.21
  593.9 9.7 collective-permute-start.23
  605.8 9.7 collective-permute-start.25
  617.7 9.7 collective-permute-start.27
  629.6 9.7 collective-permute-start.29
  641.4 9.7 collective-permute-start.31
  653.3 10.1 collective-permute-start.33
  (15 other events, 1948.1 us)
Sparse Core Ops, SparseCore 0:
  20.0 417.4 reduce-scatter.2
  439.9 24.2 reduce-scatter.4
  665.3 420.2 all-gather.1
where the time goes:
time: 1100 us; the launch traced here: 1090 us
  waiting for transfers between devices  952 us (87%)
  starting transfers between devices  96.4 us (9%)
  other arithmetic  15.4 us (1%)
  between operations  15 us (1%)
  local copies, waits for them, and re-layouts  12.8 us (1%)
    all_gather x1, waiting for transfers between devices, shards(): shard_rows = lax.all_gather(surface, ('comp', 'dom'), axis=1, tiled=True)  420 us
    reduce_scatter x1, waiting for transfers between devices, shards(): lax.psum_scatter(dense_terms, 'dom', scatter_dimension=0, tiled=True)  404 us
    ppermute x18, waiting for transfers between devices, with_halo(): lax.ppermute(lax.slice_in_dim(block, 0, width, axis=dim), axis, backward)  101 us
    ppermute x18, starting transfers between devices, with_halo(): lax.ppermute(lax.slice_in_dim(block, block.shape[dim] - width, None, axis...  52.3 us
    ppermute x18, starting transfers between devices, with_halo(): lax.ppermute(lax.slice_in_dim(block, 0, width, axis=dim), axis, backward)  44.1 us
    reduce_scatter x1, waiting for transfers between devices, shards(): lax.psum_scatter(block_sums, 'comp', scatter_dimension=0, tiled=True)  26.5 us
  transfers between devices with their start and end apart: 39, of which 18 were waited for; matrix products, arithmetic and copies ran while one was open for 1% of the time, Pallas kernels for 0%

commit v1 on v0

--- a/solution.py
+++ b/solution.py
@@ -137,7 +137,12 @@
         explicit = explicit.at[0].add(heating_gain * heating * wet)
         advected_quantity = vertical_solve(explicit, diffusivity_coefficient)
     surface = jnp.stack([advected_quantity[0], height]).astype(jnp.bfloat16)
-    shard_rows = lax.all_gather(surface, ("comp", "dom"), axis=1, tiled=True)
+    shard_rows = jnp.concatenate(
+        lax.all_to_all(
+            jnp.stack([surface] * lax.axis_size(("comp", "dom"))), ("comp", "dom"), 0, 0
+        ),
+        axis=1,
+    )
     count_rows = shard_rows.shape[1]
     selector = (targets[:, None] == jnp.arange(count_rows, dtype=jnp.int32)[None, :]).astype(
         jnp.bfloat16

time: 1100 us -> 1160 us (1.055)
  starting transfers between devices: 96.4 us -> 145 us
  waiting for transfers between devices: 952 us -> 975 us
    unnamed x3 -> x4, waiting for transfers between devices: 0.05 us -> 838 us
    reduce_scatter x2 -> x0, waiting for transfers between devices: 431 us -> none  [the longest x1 404 us: shards(): lax.psum_scatter(dense_terms, 'dom', scatter_dimension=0, tiled=True)]
    all_gather x1 -> x0, waiting for transfers between devices: 420 us -> none  [shards(): shard_rows = lax.all_gather(surface, ('comp', 'dom'), axis=1, tiled=True)]
    all_to_all x0 -> x1, starting transfers between devices: none -> 49 us  [shards(): lax.all_to_all(jnp.stack([surface] * lax.axis_size(('comp', 'dom'))), ('c...]
    all_to_all x0 -> x1, waiting for transfers between devices: none -> 30.6 us  [shards(): lax.all_to_all(jnp.stack([surface] * lax.axis_size(('comp', 'dom'))), ('c...]
where the time goes in v1:
time: 1160 us
  waiting for transfers between devices  975 us (84%)
  starting transfers between devices  145 us (12%)
  between operations  16.7 us (1%)
    unnamed x4, waiting for transfers between devices  838 us
    ppermute x18, waiting for transfers between devices, with_halo(): lax.ppermute(lax.slice_in_dim(block, 0, width, axis=dim), axis, backward)  106 us
    ppermute x18, starting transfers between devices, with_halo(): lax.ppermute(lax.slice_in_dim(block, block.shape[dim] - width, None, axis...  52 us
    all_to_all x1, starting transfers between devices, shards(): lax.all_to_all(jnp.stack([surface] * lax.axis_size(('comp', 'dom'))), ('c...  49 us
    ppermute x18, starting transfers between devices, with_halo(): lax.ppermute(lax.slice_in_dim(block, 0, width, axis=dim), axis, backward)  44.1 us
    all_to_all x1, waiting for transfers between devices, shards(): lax.all_to_all(jnp.stack([surface] * lax.axis_size(('comp', 'dom'))), ('c...  30.6 us
  transfers between devices with their start and end apart: 39, of which 18 were waited for; matrix products, arithmetic and copies ran while one was open for 1% of the time, Pallas kernels for 0%

profile of v1, /device:TPU:1, one launch (start us, length us, event | category | flops | bytes accessed | tf_op | source)
XLA Modules:
  0.0 1158.8 jit_solution(3629796743667284304)
XLA Ops:
  11.7 3.6 scatter_fusion
  15.4 5.1 collective-permute-start.16
  20.6 7.0 collective-permute-start.17
  28.9 790.8 %all-reduce.5.cloned.1.call-done = f32[2048,4,128]{2,1,0:T(4,128)} async-done(((f32[2048,4,128]{2,1,0:T(4,128)}), f32[2048,4,128]{2,1,0:T(4,128)}) %all-reduce.5.cloned.1.call-update) | async-done | bytes 4194320
  822.8 47.2 %all-reduce.7.cloned.1.call-done = f32[32,4,128]{2,1,0:T(4,128)} async-done(((f32[32,4,128]{2,1,0:T(4,128)}), f32[32,4,128]{2,1,0:T(4,128)}) %all-reduce.7.cloned.1.call-update) | async-done | bytes 65552
  870.9 7.2 collective-permute-start
  880.4 6.5 collective-permute-done.1
  889.1 2.4 collective-permute-start.3
  891.7 6.3 collective-permute-done.3
  900.1 2.4 collective-permute-start.5
  902.6 6.3 collective-permute-done.5
  911.1 2.4 collective-permute-start.7
  913.7 7.2 collective-permute-done.7
  923.0 2.4 collective-permute-start.9
  925.5 7.2 collective-permute-done.9
  934.9 2.4 collective-permute-start.11
  937.4 7.2 collective-permute-done.11
  946.8 2.4 collective-permute-start.13
  949.3 7.2 collective-permute-done.13
  958.6 2.4 collective-permute-start.15
  961.2 7.2 collective-permute-done.15
  976.3 8.0 collective-permute-start.35
  984.6 2.4 collective-permute-start.20
  989.1 7.6 collective-permute-done.21
  1001.4 7.2 collective-permute-done.23
  1013.3 7.2 collective-permute-done.25
  1025.2 7.2 collective-permute-done.27
  1037.1 7.2 collective-permute-done.29
  1048.9 7.2 collective-permute-done.31
  1060.8 7.6 collective-permute-done.33
  1070.7 49.0 %all-to-all-start = ((bf16[256,2,8,128]{3,2,1,0:T(8,128)(2,1)}), bf16[256,2,8,128]{3,2,1,0:T(8,128)(2,1)S(1)}, u32[]{:S(2)}, u32[]{:S(2)}) async-start(bf16[256,2,8,128]{3,2,1,0:T(8,128)(2,1)} %stack.158), calls=%async_computation | async-start | bytes 2097152 | tf_op jit(solution)/shard_map/all_to_all | solution.py:141
  1120.1 30.6 %all-to-all-done = bf16[256,2,8,128]{3,2,1,0:T(8,128)(2,1)S(1)} async-done(((bf16[256,2,8,128]{3,2,1,0:T(8,128)(2,1)}), bf16[256,2,8,128]{3,2,1,0:T(8,128)(2,1)S(1)}, u32[]{:S(2)}, u32[]{:S(2)}) %all-to-all-start) | async-done | bytes 1048608 | tf_op jit(solution)/shard_map/all_to_all | solution.py:141
  (305 shorter events, 68.5 us)
Async XLA Ops:
  7.2 812.5 %all-reduce.5.cloned.1.call-start = ((), (), s32[]{:S(2)}) async-start(), calls=%async_computation.1 | async-start | bytes 8388608
  15.4 854.6 %all-reduce.7.cloned.1.call-start = ((), (), s32[]{:S(2)}) async-start(), calls=%async_computation.2 | async-start | bytes 131072
  15.4 952.9 %collective-permute-start.16 = (f32[32,1,128]{2,1,0:T(1,128)S(1)}, f32[32,1,128]{2,1,0:T(1,128)S(1)}, u32[]{:S(2)}, u32[]{:S(2)}) collective-permute-start(f32[32,1,128]{2,1,0:T(1,128)S(1)} %get-tuple-element.179), channel_id=1, source_target_pairs={{1,0},{2,1},{3,2},{4,3},{5,4},{6,5},{7,6},{8,7},{9,8},{10,9},{11,1... | collective-permute-start | bytes 49160 | tf_op jit(solution)/shard_map/ppermute | solution.py:23
  20.6 947.8 %collective-permute-start.17 = (f32[32,1,128]{2,1,0:T(1,128)S(1)}, f32[32,1,128]{2,1,0:T(1,128)S(1)}, u32[]{:S(2)}, u32[]{:S(2)}) collective-permute-start(f32[32,1,128]{2,1,0:T(1,128)S(1)} %get-tuple-element.178), channel_id=1, source_target_pairs={{0,1},{1,2},{2,3},{3,4},{4,5},{5,6},{6,7},{7,8},{8,9},{9,10},{10,1... | collective-permute-start | bytes 49160 | tf_op jit(solution)/shard_map/ppermute | solution.py:20
  870.9 9.5 collective-permute-start
  878.1 8.8 collective-permute-start.1
  887.2 4.5 collective-permute-start.2
  889.1 8.8 collective-permute-start.3
  898.1 4.5 collective-permute-start.4
  900.1 8.8 collective-permute-start.5
  909.2 4.5 collective-permute-start.6
  911.1 9.7 collective-permute-start.7
  921.0 4.5 collective-permute-start.8
  923.0 9.7 collective-permute-start.9
  932.9 4.5 collective-permute-start.10
  934.9 9.7 collective-permute-start.11
  944.8 4.5 collective-permute-start.12
  946.8 9.7 collective-permute-start.13
  958.6 9.7 collective-permute-start.15
  969.7 14.6 %collective-permute-start.18 = (f32[4,1,128]{2,1,0:T(1,128)S(1)}, f32[4,1,128]{2,1,0:T(1,128)S(1)}, u32[]{:S(2)}, u32[]{:S(2)}) collective-permute-start(f32[4,1,128]{2,1,0:T(1,128)S(1)} %get-tuple-element.215), channel_id=1, source_target_pairs={{0,1},{1,2},{2,3},{3,4},{4,5},{5,6},{6,7},{7,8},{8,9},{9,10},{10,1... | collective-permute-start | bytes 6152 | tf_op jit(solution)/shard_map/ppermute | solution.py:20
  971.7 12.7 %collective-permute-start.19 = (f32[4,1,128]{2,1,0:T(1,128)S(1)}, f32[4,1,128]{2,1,0:T(1,128)S(1)}, u32[]{:S(2)}, u32[]{:S(2)}) collective-permute-start(f32[4,1,128]{2,1,0:T(1,128)S(1)} %get-tuple-element.214), channel_id=1, source_target_pairs={{1,0},{2,1},{3,2},{4,3},{5,4},{6,5},{7,6},{8,7},{9,8},{10,9},{11,1... | collective-permute-start | bytes 6152 | tf_op jit(solution)/shard_map/ppermute | solution.py:23
  974.4 94.7 %collective-permute-start.34 = (f32[32,1,128]{2,1,0:T(1,128)S(1)}, f32[32,1,128]{2,1,0:T(1,128)S(1)}, u32[]{:S(2)}, u32[]{:S(2)}) collective-permute-start(f32[32,1,128]{2,1,0:T(1,128)S(1)} %get-tuple-element.177), channel_id=1, source_target_pairs={{1,0},{2,1},{3,2},{4,3},{5,4},{6,5},{7,6},{8,7},{9,8},{10,9},{11,1... | collective-permute-start | bytes 49160 | tf_op jit(solution)/shard_map/ppermute | solution.py:23
  976.3 92.8 %collective-permute-start.35 = (f32[32,1,128]{2,1,0:T(1,128)S(1)}, f32[32,1,128]{2,1,0:T(1,128)S(1)}, u32[]{:S(2)}, u32[]{:S(2)}) collective-permute-start(f32[32,1,128]{2,1,0:T(1,128)S(1)} %get-tuple-element.176), channel_id=1, source_target_pairs={{0,1},{1,2},{2,3},{3,4},{4,5},{5,6},{6,7},{7,8},{8,9},{9,10},{10,1... | collective-permute-start | bytes 49160 | tf_op jit(solution)/shard_map/ppermute | solution.py:20
  984.6 4.5 collective-permute-start.20
  987.0 9.7 collective-permute-start.21
  998.9 9.7 collective-permute-start.23
  1010.8 9.7 collective-permute-start.25
  1022.6 9.7 collective-permute-start.27
  1034.5 9.7 collective-permute-start.29
  1046.4 9.7 collective-permute-start.31
  1058.3 10.1 collective-permute-start.33
  1070.7 80.0 %all-to-all-start = ((bf16[256,2,8,128]{3,2,1,0:T(8,128)(2,1)}), bf16[256,2,8,128]{3,2,1,0:T(8,128)(2,1)S(1)}, u32[]{:S(2)}, u32[]{:S(2)}) async-start(bf16[256,2,8,128]{3,2,1,0:T(8,128)(2,1)} %stack.158), calls=%async_computation | async-start | bytes 2097152 | tf_op jit(solution)/shard_map/all_to_all | solution.py:141
  (16 other events, 4291.4 us)
Sparse Core Ops, SparseCore 0:
  15.5 804.1 all-reduce.4
  822.9 47.0 all-reduce.6
